TPU v7x, 128 devices: a whole 4x4x4 slice. The times are simulated.
128 devices in a mesh: row: 8 (over y, core), col: 16 (over x, z).
Axes of the slice: x: 4, y: 4, z: 4, core: 2. Of those that a mesh axis runs over, the one named last changes fastest.
Arguments:
- tokens: bfloat16 [2048, 8192], P('col', 'row'), may hold values from -6 to 6
- gate_weight: bfloat16 [8192, 28672], P('row', 'col'), may hold values from -0.109375 to 0.109375
- up_weight: bfloat16 [8192, 28672], P('row', 'col'), may hold values from -0.109375 to 0.109375
- down_weight: bfloat16 [28672, 8192], P('col', 'row'), may hold values from -0.0546875 to 0.0546875
- gate_keep: int32 [224, 48], P('col'), may hold values from 0 to 63, as said below
- gate_count: int32 [224], P('col'), may hold values from 5 to 48, as said below
- up_keep: int32 [224, 48], P('col'), may hold values from 0 to 63, as said below
- up_count: int32 [224], P('col'), may hold values from 5 to 48, as said below
- down_keep: int32 [64, 176], P('row'), may hold values from 0 to 223, as said below
- down_count: int32 [64], P('row'), may hold values from 15 to 176, as said below
Outputs:
- output_rows: bfloat16 [2048, 8192], P('col', 'row')
Inputs may be any that keep to these rules, and one draw needn't show every extreme that they name: `gate_keep`: each row holds distinct block indices of the model features. `gate_count`: some block column uses all 48 slots. `up_keep`: each row holds distinct block indices of the model features. `up_count`: some block column uses all 48 slots. `down_keep`: each row holds distinct block indices of the hidden units. `down_count`: some block column uses all 176 slots.
All inputs are finite; a program needn't handle non-finite values.
Results may differ from a plain program's by a relative error of at most 0.028.
Values may be sent and summed in bfloat16 or wider, within the bound.
A program may use at most 128 MiB of HBM per device.

v0:
```python
import jax
import jax.numpy as jnp
from jax import lax
from jax.sharding import PartitionSpec as P

BLOCK = 128
CHUNKS = 1
COL_A2A = True
COL_RING = False


def local_mask(keep_list, keep_count, offset, blocks):
    position = jnp.arange(keep_list.shape[1], dtype=jnp.int32)
    active_slot = position[None, :] < keep_count[:, None]
    local_index = keep_list - offset
    matches = (
        local_index[:, :, None] == jnp.arange(blocks, dtype=jnp.int32)[None, None, :]
    ) & active_slot[:, :, None]
    return jnp.any(matches, axis=1)


def apply_mask(weight, block_mask, block_size):
    block_rows, block_cols = block_mask.shape
    shaped = weight.reshape(block_rows, block_size, block_cols, block_size)
    masked = jnp.where(block_mask[:, None, :, None], shaped, jnp.zeros((), weight.dtype))
    return masked.reshape(weight.shape)


def row_perm(n_row, step):
    n_y = n_row // 2
    return [(y * 2 + c, (y + step) % n_y * 2 + c) for y in range(n_y) for c in range(2)]


def row_reduce_scatter(tokens, weights, n_row, after):
    n_y = n_row // 2
    r = lax.axis_index("row")
    y = r // 2
    core = r % 2
    rows = tokens.shape[0]
    width = weights.shape[1]
    halves = tokens.reshape(2, rows // 2, tokens.shape[1])
    send = lax.dynamic_index_in_dim(halves, 1 - core, 0, keepdims=False)
    keep = lax.dynamic_index_in_dim(halves, core, 0, keepdims=False)
    send = jnp.dot(send, weights, preferred_element_type=jnp.float32).astype(jnp.bfloat16)
    swap = [(i, i ^ 1) for i in range(n_row)]
    got = lax.ppermute(send, "row", swap)
    keep = jnp.dot(keep, weights, preferred_element_type=jnp.float32).astype(jnp.bfloat16)
    pair = (keep.astype(jnp.float32) + got.astype(jnp.float32)).astype(jnp.bfloat16)
    if after is not None:
        pair, after = lax.optimization_barrier((pair, after))
    chunk = rows // 2 // n_y
    pair = pair.reshape(n_y, chunk, width)
    results = []
    for direction, cols in ((1, slice(0, width // 2)), (-1, slice(width // 2, width))):
        own = pair[:, :, cols]
        index = (y - direction) % n_y
        acc = lax.dynamic_index_in_dim(own, index, 0, keepdims=False)
        for step in range(n_y - 1):
            got = lax.ppermute(acc.astype(jnp.bfloat16), "row", row_perm(n_row, direction))
            index = (index - direction) % n_y
            acc = got.astype(jnp.float32) + lax.dynamic_index_in_dim(own, index, 0, keepdims=False)
        results.append(acc)
    return results


def row_all_gather(value, n_row):
    n_y = n_row // 2
    r = lax.axis_index("row")
    y = r // 2
    core = r % 2
    chunk, width = value.shape
    parts = []
    for direction, cols in ((1, slice(0, width // 2)), (-1, slice(width // 2, width))):
        held = value[:, cols]
        full = jnp.zeros((n_y, chunk, width // 2), value.dtype)
        full = lax.dynamic_update_index_in_dim(full, held, y, 0)
        for step in range(n_y - 1):
            held = lax.ppermute(held, "row", row_perm(n_row, direction))
            full = lax.dynamic_update_index_in_dim(
                full, held, (y - direction * (step + 1)) % n_y, 0
            )
        parts.append(full)
    half = jnp.concatenate(parts, axis=2).reshape(n_y * chunk, width)
    swap = [(i, i ^ 1) for i in range(n_row)]
    other = lax.ppermute(half, "row", swap)
    both = jnp.zeros((2, n_y * chunk, width), value.dtype)
    both = lax.dynamic_update_index_in_dim(both, half, core, 0)
    both = lax.dynamic_update_index_in_dim(both, other, 1 - core, 0)
    return both.reshape(2 * n_y * chunk, width)


def ring_reduce_scatter(own, pos, n, perm_of):
    width = own.shape[2]
    halves = []
    for direction, cols in ((1, slice(0, width // 2)), (-1, slice(width // 2, width))):
        part = own[:, :, cols]
        index = (pos - direction) % n
        acc = lax.dynamic_index_in_dim(part, index, 0, keepdims=False).astype(jnp.float32)
        for step in range(n - 1):
            got = lax.ppermute(acc.astype(jnp.bfloat16), "col", perm_of(direction))
            index = (index - direction) % n
            acc = got.astype(jnp.float32) + lax.dynamic_index_in_dim(part, index, 0, keepdims=False)
        halves.append(acc)
    return jnp.concatenate(halves, axis=1)


def ring_all_gather(value, pos, n, perm_of):
    chunk, width = value.shape
    parts = []
    for direction, cols in ((1, slice(0, width // 2)), (-1, slice(width // 2, width))):
        held = value[:, cols]
        full = jnp.zeros((n, chunk, width // 2), value.dtype)
        full = lax.dynamic_update_index_in_dim(full, held, pos, 0)
        for step in range(n - 1):
            held = lax.ppermute(held, "col", perm_of(direction))
            full = lax.dynamic_update_index_in_dim(
                full, held, (pos - direction * (step + 1)) % n, 0
            )
        parts.append(full)
    return jnp.concatenate(parts, axis=2)


def col_axes(n_col):
    n_z = 4 if n_col % 4 == 0 else 1
    n_x = n_col // n_z
    c = lax.axis_index("col")

    def x_perm(d):
        return [(i * n_z + j, (i + d) % n_x * n_z + j) for i in range(n_x) for j in range(n_z)]

    def z_perm(d):
        return [(i * n_z + j, i * n_z + (j + d) % n_z) for i in range(n_x) for j in range(n_z)]

    return (n_x, n_z, c // n_z, c % n_z, x_perm, z_perm)


def col_all_gather(value, n_col):
    n_x, n_z, x, z, x_perm, z_perm = col_axes(n_col)
    rows, width = value.shape
    part = ring_all_gather(value, z, n_z, z_perm).reshape(n_z * rows, width)
    return ring_all_gather(part, x, n_x, x_perm).reshape(n_x * n_z * rows, width)


def col_reduce_scatter(terms, n_col):
    n_z = 4 if n_col % 4 == 0 else 1
    n_x = n_col // n_z
    c = lax.axis_index("col")
    x = c // n_z
    z = c % n_z
    rows, width = terms.shape

    def x_perm(d):
        return [(i * n_z + j, (i + d) % n_x * n_z + j) for i in range(n_x) for j in range(n_z)]

    def z_perm(d):
        return [(i * n_z + j, i * n_z + (j + d) % n_z) for i in range(n_x) for j in range(n_z)]

    part = ring_reduce_scatter(terms.reshape(n_x, rows // n_x, width), x, n_x, x_perm)
    part = part.astype(jnp.bfloat16).reshape(n_z, rows // n_x // n_z, width)
    return ring_reduce_scatter(part, z, n_z, z_perm).astype(jnp.bfloat16)


def on_device(
    tokens,
    gate_weight,
    up_weight,
    down_weight,
    gate_keep,
    gate_count,
    up_keep,
    up_count,
    down_keep,
    down_count,
):
    model_blocks = gate_weight.shape[0] // BLOCK
    hidden_blocks = gate_weight.shape[1] // BLOCK
    n_col = lax.axis_size("col")
    n_row = lax.axis_size("row")
    row_offset = lax.axis_index("row") * model_blocks
    col_offset = lax.axis_index("col") * hidden_blocks
    gate_pruned = apply_mask(
        gate_weight, local_mask(gate_keep, gate_count, row_offset, model_blocks).T, BLOCK
    )
    up_pruned = apply_mask(
        up_weight, local_mask(up_keep, up_count, row_offset, model_blocks).T, BLOCK
    )
    down_pruned = apply_mask(
        down_weight, local_mask(down_keep, down_count, col_offset, hidden_blocks).T, BLOCK
    )
    both_weights = jnp.concatenate([gate_pruned, up_pruned], axis=1)
    rows = tokens.shape[0] // CHUNKS
    gathered = lax.all_gather(tokens, "col", axis=0, tiled=True)
    gathered = gathered.reshape(n_col, CHUNKS, rows, gathered.shape[1])
    outs = []
    previous = None
    for k in range(CHUNKS):
        chunk = gathered[:, k].reshape(n_col * rows, gathered.shape[3])
        gate_sums, up_sums = row_reduce_scatter(chunk, both_weights, n_row, previous)
        hidden = (jax.nn.silu(gate_sums) * up_sums).astype(jnp.bfloat16)
        hidden = row_all_gather(hidden, n_row)
        terms = jnp.dot(hidden, down_pruned, preferred_element_type=jnp.float32).astype(
            jnp.bfloat16
        )
        previous = terms
        if COL_RING:
            outs.append(col_reduce_scatter(terms, n_col))
        elif COL_A2A and k == CHUNKS - 1:
            split = terms.shape[1] // 2
            left = lax.psum_scatter(terms[:, :split], "col", scatter_dimension=0, tiled=True)
            right = terms[:, split:].reshape(n_col, rows, terms.shape[1] - split)
            right = lax.all_to_all(right, "col", 0, 0, tiled=False)
            right = jnp.sum(right.astype(jnp.float32), axis=0).astype(jnp.bfloat16)
            outs.append(jnp.concatenate([left, right], axis=1))
        else:
            outs.append(lax.psum_scatter(terms, "col", scatter_dimension=0, tiled=True))
    return jnp.concatenate(outs, axis=0)


def solution(mesh):
    return jax.shard_map(
        on_device,
        mesh=mesh,
        in_specs=(
            P("col", "row"),
            P("row", "col"),
            P("row", "col"),
            P("col", "row"),
            P("col", None),
            P("col"),
            P("col", None),
            P("col"),
            P("row", None),
            P("row"),
        ),
        out_specs=P("col", "row"),
        check_vma=False,
    )
```

profile of v0, /device:TPU:0, one launch (start us, length us, event | category | flops | bytes accessed | tf_op | source)
XLA Modules:
  0.0 336.2 jit_solution(16218142034892544650)
XLA Ops:
  7.3 6.0 %copy.14 = bf16[1024,1792]{0,1:T(8,128)(2,1)} copy(bf16[1024,1792]{1,0:T(8,128)(2,1)} %param.12) | data formatting | bytes 7340032 | tf_op args[2]
  13.3 6.0 %copy.13 = bf16[1024,1792]{0,1:T(8,128)(2,1)} copy(bf16[1024,1792]{1,0:T(8,128)(2,1)} %param.11) | data formatting | bytes 7340032 | tf_op args[1]
  20.7 5.1 %bitcast_select_fusion.1 = bf16[1024,1792]{0,1:T(8,128)(2,1)} fusion(bf16[1024,1792]{0,1:T(8,128)(2,1)} %copy.14, pred[224,8,8,128]{3,2,1,0:T(8,128)(4,1)S(1)} %bitcast.78), kind=kLoop, calls=%fused_computation.5 | loop fusion | flops 1835008 | bytes 9175040 | tf_op jit(solution)/shard_map/jit(_where)/select_n | solution.py:25
  29.2 34.3 %all-gather.2.cloned.1.call-done = bf16[2048,1024]{1,0:T(8,128)(2,1)} async-done(((bf16[128,1024]{1,0:T(8,128)(2,1)}), bf16[2048,1024]{1,0:T(8,128)(2,1)}) %all-gather.2.cloned.1.call-update) | async-done | bytes 4194320 | tf_op jit(solution)/shard_map/all_gather | solution.py:192
  63.5 13.4 %convolution_convert_fusion = bf16[1024,3584]{1,0:T(8,128)(2,1)} fusion(bf16[1024,1792]{0,1:T(8,128)(2,1)} %bitcast_select_fusion.1, bf16[1024,1792]{0,1:T(8,128)(2,1)} %bitcast_select_fusion.2, bf16[2,1024,1024]{2,1,0:T(8,128)(2,1)} %bitcast.84, s32[]{:T(128)S(6)} %select_n.138), kind=kOutput, calls=%fused_computation.1 | convolution fusion | flops 7534542848 | bytes 16777220 | tf_op jit(solution)/shard_map/dot_general | solution.py:44
  76.9 12.0 %collective-permute-done = bf16[1024,3584]{1,0:T(8,128)(2,1)} collective-permute-done((bf16[1024,3584]{1,0:T(8,128)(2,1)}, bf16[1024,3584]{1,0:T(8,128)(2,1)}, u32[]{:S(2)}, u32[]{:S(2)}) %collective-permute-start) | collective-permute-done | bytes 7340064 | tf_op jit(solution)/shard_map/ppermute | solution.py:46
  88.9 14.5 %add_convert_fusion = bf16[1024,3584]{1,0:T(8,128)(2,1)} fusion(bf16[1024,3584]{1,0:T(8,128)(2,1)} %collective-permute-done, bf16[1024,1792]{0,1:T(8,128)(2,1)} %bitcast_select_fusion.1, bf16[1024,1792]{0,1:T(8,128)(2,1)} %bitcast_select_fusion.2, bf16[2,1024,1024]{2,1,0:T(8,128)(2,1)} %bitcast.85, s32[]{:T(128)S(6)} %select_n.135), kind=kOutput, calls=%fused_computation | convolution fusion | flops 7549222912 | bytes 24117252 | tf_op jit(solution)/shard_map/dot_general | solution.py:47
  103.4 5.4 %fusion.22 = (bf16[4,256,1792]{2,1,0:T(8,128)(2,1)S(1)}, bf16[4,256,1792]{2,1,0:T(8,128)(2,1)}) fusion(bf16[4,256,3584]{2,1,0:T(8,128)(2,1)} %bitcast.76), kind=kLoop, calls=%fused_computation.59 | loop fusion | bytes 14680064 | tf_op jit(solution)/shard_map/slice | solution.py:55
  116.2 18.1 %collective-permute-done.1 = bf16[256,1792]{1,0:T(8,128)(2,1)S(1)} collective-permute-done((bf16[256,1792]{1,0:T(8,128)(2,1)S(1)}, bf16[256,1792]{1,0:T(8,128)(2,1)S(1)}, u32[]{:S(2)}, u32[]{:S(2)}) %collective-permute-start.1) | collective-permute-done | bytes 917536 | tf_op jit(solution)/shard_map/ppermute | solution.py:59
  139.2 3.0 collective-permute-start.5
  142.2 16.4 %collective-permute-done.2 = bf16[256,1792]{1,0:T(8,128)(2,1)S(1)} collective-permute-done((bf16[256,1792]{1,0:T(8,128)(2,1)S(1)}, bf16[256,1792]{1,0:T(8,128)(2,1)S(1)}, u32[]{:S(2)}, u32[]{:S(2)}) %collective-permute-start.2) | collective-permute-done | bytes 917536 | tf_op jit(solution)/shard_map/ppermute | solution.py:59
  163.9 3.7 %collective-permute-start.6 = (bf16[256,1792]{1,0:T(8,128)(2,1)}, bf16[256,1792]{1,0:T(8,128)(2,1)S(1)}, u32[]{:S(2)}, u32[]{:S(2)}) collective-permute-start(bf16[256,1792]{1,0:T(8,128)(2,1)} %fusion.6), channel_id=1, source_target_pairs={{0,96},{16,112},{32,0},{48,16},{64,32},{80,48},{96,64},{112,80},{1... | collective-permute-start | bytes 2752520 | tf_op jit(solution)/shard_map/ppermute | solution.py:59
  167.6 14.3 %collective-permute-done.3 = bf16[256,1792]{1,0:T(8,128)(2,1)S(1)} collective-permute-done((bf16[256,1792]{1,0:T(8,128)(2,1)S(1)}, bf16[256,1792]{1,0:T(8,128)(2,1)S(1)}, u32[]{:S(2)}, u32[]{:S(2)}) %collective-permute-start.3) | collective-permute-done | bytes 917536 | tf_op jit(solution)/shard_map/ppermute | solution.py:59
  181.9 3.9 %collective-permute-done.6 = bf16[256,1792]{1,0:T(8,128)(2,1)S(1)} collective-permute-done((bf16[256,1792]{1,0:T(8,128)(2,1)}, bf16[256,1792]{1,0:T(8,128)(2,1)S(1)}, u32[]{:S(2)}, u32[]{:S(2)}) %collective-permute-start.6) | collective-permute-done | bytes 917536 | tf_op jit(solution)/shard_map/ppermute | solution.py:59
  188.2 3.7 %collective-permute-start.10 = (bf16[256,896]{1,0:T(8,128)(2,1)S(1)}, bf16[256,896]{1,0:T(8,128)(2,1)S(1)}, u32[]{:S(2)}, u32[]{:S(2)}) collective-permute-start(bf16[256,896]{1,0:T(8,128)(2,1)S(1)} %get-tuple-element.10), channel_id=1, source_target_pairs={{0,96},{16,112},{32,0},{48,16},{64,32},{80,48},{96,64},{112,80},{1... | collective-permute-start | bytes 1376264 | tf_op jit(solution)/shard_map/ppermute | solution.py:78
  192.3 7.5 %collective-permute-done.7 = bf16[256,896]{1,0:T(8,128)(2,1)S(1)} collective-permute-done((bf16[256,896]{1,0:T(8,128)(2,1)S(1)}, bf16[256,896]{1,0:T(8,128)(2,1)S(1)}, u32[]{:S(2)}, u32[]{:S(2)}) %collective-permute-start.7) | collective-permute-done | bytes 458784 | tf_op jit(solution)/shard_map/ppermute | solution.py:78
  199.8 3.2 collective-permute-start.11
  203.1 7.3 %collective-permute-done.8 = bf16[256,896]{1,0:T(8,128)(2,1)S(1)} collective-permute-done((bf16[256,896]{1,0:T(8,128)(2,1)S(1)}, bf16[256,896]{1,0:T(8,128)(2,1)S(1)}, u32[]{:S(2)}, u32[]{:S(2)}) %collective-permute-start.8) | collective-permute-done | bytes 458784 | tf_op jit(solution)/shard_map/ppermute | solution.py:78
  210.5 3.2 collective-permute-start.12
  213.8 6.3 %collective-permute-done.9 = bf16[256,896]{1,0:T(8,128)(2,1)S(1)} collective-permute-done((bf16[256,896]{1,0:T(8,128)(2,1)S(1)}, bf16[256,896]{1,0:T(8,128)(2,1)S(1)}, u32[]{:S(2)}, u32[]{:S(2)}) %collective-permute-start.9) | collective-permute-done | bytes 458784 | tf_op jit(solution)/shard_map/ppermute | solution.py:78
  225.7 3.4 %collective-permute-done.13 = bf16[1024,1792]{1,0:T(8,128)(2,1)} collective-permute-done((bf16[1024,1792]{1,0:T(8,128)(2,1)}, bf16[1024,1792]{1,0:T(8,128)(2,1)}, u32[]{:S(2)}, u32[]{:S(2)}) %collective-permute-start.13) | collective-permute-done | bytes 3670048 | tf_op jit(solution)/shard_map/ppermute | solution.py:85
  232.1 8.2 %convolution_convert_fusion.2 = bf16[2048,1024]{1,0:T(8,128)(2,1)S(1)} fusion(bf16[2048,1792]{1,0:T(8,128)(2,1)S(1)} %bitcast.77, bf16[1792,1024]{1,0:T(8,128)(2,1)S(1)} %copy-done.8, pred[224,8,8,128]{3,2,1,0:T(8,128)(4,1)S(1)} %bitcast.80), kind=kOutput, calls=%fused_computation.7 | convolution fusion | flops 7520124928 | bytes 17039360 | tf_op jit(solution)/shard_map/dot_general | solution.py:201
  242.7 37.1 %all_to_all.5 = bf16[16,128,512]{2,1,0:T(8,128)(2,1)S(1)} all-to-all(bf16[16,128,512]{2,1,0:T(8,128)(2,1)} %bitcast.75), channel_id=1, replica_groups=mesh['row'=8,'col'=16] {'col'}, dimensions={0} | all-to-all | bytes 4194304 | tf_op jit(solution)/shard_map/all_to_all | solution.py:211
  280.1 47.7 %reduce-scatter.2.cloned.1.call-done = bf16[128,512]{1,0:T(8,128)(2,1)} async-done(((bf16[2048,512]{1,0:T(8,128)(2,1)}), bf16[128,512]{1,0:T(8,128)(2,1)}) %reduce-scatter.2.cloned.1.call-update) | async-done | bytes 131088 | tf_op jit(solution)/shard_map/reduce_scatter | solution.py:209
  (73 shorter events, 38.8 us)
Async XLA Ops:
  6.5 57.0 %all-gather.2.cloned.1.call-start = ((), (), s32[]{:S(2)}) async-start(), calls=%async_computation.2 | async-start | bytes 4456448 | tf_op jit(solution)/shard_map/all_gather | solution.py:192
  7.3 320.5 %reduce-scatter.2.cloned.1.call-start = ((), (), s32[]{:S(2)}) async-start(), calls=%async_computation.3 | async-start | bytes 2228224 | tf_op jit(solution)/shard_map/reduce_scatter | solution.py:209
  13.3 6.0 %copy-start.5 = (s32[14]{0:T(128)S(1)}, s32[14]{0:T(128)}, u32[]{:S(2)}) copy-start(s32[14]{0:T(128)} %param.17) | copy-start | bytes 172
  13.3 6.1 %copy-start.3 = (s32[14,48]{1,0:T(8,128)S(1)}, s32[14,48]{1,0:T(8,128)}, u32[]{:S(2)}) copy-start(s32[14,48]{1,0:T(8,128)} %param.16) | copy-start | bytes 8068
  13.3 6.1 %copy-start.4 = (s32[14,48]{1,0:T(8,128)S(1)}, s32[14,48]{1,0:T(8,128)}, u32[]{:S(2)}) copy-start(s32[14,48]{1,0:T(8,128)} %param.14) | copy-start | bytes 8068
  13.3 6.4 %copy-start.6 = (s32[14]{0:T(128)S(1)}, s32[14]{0:T(128)}, u32[]{:S(2)}) copy-start(s32[14]{0:T(128)} %param.15) | copy-start | bytes 172
  20.7 5.7 %copy-start.1 = (bf16[1024,1792]{0,1:T(8,128)(2,1)S(1)}, bf16[1024,1792]{0,1:T(8,128)(2,1)}, u32[]{:S(2)}) copy-start(bf16[1024,1792]{0,1:T(8,128)(2,1)} %copy.13) | copy-start | bytes 11010052
  76.9 12.0 %collective-permute-start = (bf16[1024,3584]{1,0:T(8,128)(2,1)}, bf16[1024,3584]{1,0:T(8,128)(2,1)}, u32[]{:S(2)}, u32[]{:S(2)}) collective-permute-start(bf16[1024,3584]{1,0:T(8,128)(2,1)} %convolution_convert_fusion), channel_id=1, source_target_pairs={{0,16},{16,0},{32,48},{48,32},{64,80},{80,64},{96,112},{112,96},{1... | collective-permute-start | bytes 22020104 | tf_op jit(solution)/shard_map/ppermute | solution.py:46
  110.7 23.7 %collective-permute-start.1 = (bf16[256,1792]{1,0:T(8,128)(2,1)S(1)}, bf16[256,1792]{1,0:T(8,128)(2,1)S(1)}, u32[]{:S(2)}, u32[]{:S(2)}) collective-permute-start(bf16[256,1792]{1,0:T(8,128)(2,1)S(1)} %dynamic-slice_bitcast_fusion.1), channel_id=1, source_target_pairs={{0,32},{16,48},{32,64},{48,80},{64,96},{80,112},{96,0},{112,16},{1... | collective-permute-start | bytes 2752520 | tf_op jit(solution)/shard_map/ppermute | solution.py:59
  114.5 22.3 %collective-permute-start.4 = (bf16[256,1792]{1,0:T(8,128)(2,1)}, bf16[256,1792]{1,0:T(8,128)(2,1)S(1)}, u32[]{:S(2)}, u32[]{:S(2)}) collective-permute-start(bf16[256,1792]{1,0:T(8,128)(2,1)} %dynamic-slice_bitcast_fusion), channel_id=1, source_target_pairs={{0,96},{16,112},{32,0},{48,16},{64,32},{80,48},{96,64},{112,80},{1... | collective-permute-start | bytes 2752520 | tf_op jit(solution)/shard_map/ppermute | solution.py:59
  135.8 22.8 %collective-permute-start.2 = (bf16[256,1792]{1,0:T(8,128)(2,1)S(1)}, bf16[256,1792]{1,0:T(8,128)(2,1)S(1)}, u32[]{:S(2)}, u32[]{:S(2)}) collective-permute-start(bf16[256,1792]{1,0:T(8,128)(2,1)S(1)} %fusion.9), channel_id=1, source_target_pairs={{0,32},{16,48},{32,64},{48,80},{64,96},{80,112},{96,0},{112,16},{1... | collective-permute-start | bytes 2752520 | tf_op jit(solution)/shard_map/ppermute | solution.py:59
  139.2 22.0 %collective-permute-start.5 = (bf16[256,1792]{1,0:T(8,128)(2,1)}, bf16[256,1792]{1,0:T(8,128)(2,1)}, u32[]{:S(2)}, u32[]{:S(2)}) collective-permute-start(bf16[256,1792]{1,0:T(8,128)(2,1)} %fusion.7), channel_id=1, source_target_pairs={{0,96},{16,112},{32,0},{48,16},{64,32},{80,48},{96,64},{112,80},{1... | collective-permute-start | bytes 2752520 | tf_op jit(solution)/shard_map/ppermute | solution.py:59
  160.0 22.0 %collective-permute-start.3 = (bf16[256,1792]{1,0:T(8,128)(2,1)S(1)}, bf16[256,1792]{1,0:T(8,128)(2,1)S(1)}, u32[]{:S(2)}, u32[]{:S(2)}) collective-permute-start(bf16[256,1792]{1,0:T(8,128)(2,1)S(1)} %fusion.8), channel_id=1, source_target_pairs={{0,32},{16,48},{32,64},{48,80},{64,96},{80,112},{96,0},{112,16},{1... | collective-permute-start | bytes 2752520 | tf_op jit(solution)/shard_map/ppermute | solution.py:59
  163.9 21.9 %collective-permute-start.6 = (bf16[256,1792]{1,0:T(8,128)(2,1)}, bf16[256,1792]{1,0:T(8,128)(2,1)S(1)}, u32[]{:S(2)}, u32[]{:S(2)}) collective-permute-start(bf16[256,1792]{1,0:T(8,128)(2,1)} %fusion.6), channel_id=1, source_target_pairs={{0,96},{16,112},{32,0},{48,16},{64,32},{80,48},{96,64},{112,80},{1... | collective-permute-start | bytes 2752520 | tf_op jit(solution)/shard_map/ppermute | solution.py:59
  188.1 11.6 %collective-permute-start.7 = (bf16[256,896]{1,0:T(8,128)(2,1)S(1)}, bf16[256,896]{1,0:T(8,128)(2,1)S(1)}, u32[]{:S(2)}, u32[]{:S(2)}) collective-permute-start(bf16[256,896]{1,0:T(8,128)(2,1)S(1)} %get-tuple-element.9), channel_id=1, source_target_pairs={{0,32},{16,48},{32,64},{48,80},{64,96},{80,112},{96,0},{112,16},{1... | collective-permute-start | bytes 1376264 | tf_op jit(solution)/shard_map/ppermute | solution.py:78
  188.2 11.5 %collective-permute-start.10 = (bf16[256,896]{1,0:T(8,128)(2,1)S(1)}, bf16[256,896]{1,0:T(8,128)(2,1)S(1)}, u32[]{:S(2)}, u32[]{:S(2)}) collective-permute-start(bf16[256,896]{1,0:T(8,128)(2,1)S(1)} %get-tuple-element.10), channel_id=1, source_target_pairs={{0,96},{16,112},{32,0},{48,16},{64,32},{80,48},{96,64},{112,80},{1... | collective-permute-start | bytes 1376264 | tf_op jit(solution)/shard_map/ppermute | solution.py:78
  199.8 10.7 %collective-permute-start.8 = (bf16[256,896]{1,0:T(8,128)(2,1)S(1)}, bf16[256,896]{1,0:T(8,128)(2,1)S(1)}, u32[]{:S(2)}, u32[]{:S(2)}) collective-permute-start(bf16[256,896]{1,0:T(8,128)(2,1)S(1)} %collective-permute-done.7), channel_id=1, source_target_pairs={{0,32},{16,48},{32,64},{48,80},{64,96},{80,112},{96,0},{112,16},{1... | collective-permute-start | bytes 1376264 | tf_op jit(solution)/shard_map/ppermute | solution.py:78
  199.8 10.7 %collective-permute-start.11 = (bf16[256,896]{1,0:T(8,128)(2,1)S(1)}, bf16[256,896]{1,0:T(8,128)(2,1)S(1)}, u32[]{:S(2)}, u32[]{:S(2)}) collective-permute-start(bf16[256,896]{1,0:T(8,128)(2,1)S(1)} %collective-permute-done.10), channel_id=1, source_target_pairs={{0,96},{16,112},{32,0},{48,16},{64,32},{80,48},{96,64},{112,80},{1... | collective-permute-start | bytes 1376264 | tf_op jit(solution)/shard_map/ppermute | solution.py:78
  210.5 9.7 %collective-permute-start.9 = (bf16[256,896]{1,0:T(8,128)(2,1)S(1)}, bf16[256,896]{1,0:T(8,128)(2,1)S(1)}, u32[]{:S(2)}, u32[]{:S(2)}) collective-permute-start(bf16[256,896]{1,0:T(8,128)(2,1)S(1)} %collective-permute-done.8), channel_id=1, source_target_pairs={{0,32},{16,48},{32,64},{48,80},{64,96},{80,112},{96,0},{112,16},{1... | collective-permute-start | bytes 1376264 | tf_op jit(solution)/shard_map/ppermute | solution.py:78
  210.5 9.7 %collective-permute-start.12 = (bf16[256,896]{1,0:T(8,128)(2,1)S(1)}, bf16[256,896]{1,0:T(8,128)(2,1)S(1)}, u32[]{:S(2)}, u32[]{:S(2)}) collective-permute-start(bf16[256,896]{1,0:T(8,128)(2,1)S(1)} %collective-permute-done.11), channel_id=1, source_target_pairs={{0,96},{16,112},{32,0},{48,16},{64,32},{80,48},{96,64},{112,80},{1... | collective-permute-start | bytes 1376264 | tf_op jit(solution)/shard_map/ppermute | solution.py:78
  220.3 2.1 copy-start.7
  220.3 2.1 copy-start.2
  222.3 6.8 %collective-permute-start.13 = (bf16[1024,1792]{1,0:T(8,128)(2,1)}, bf16[1024,1792]{1,0:T(8,128)(2,1)}, u32[]{:S(2)}, u32[]{:S(2)}) collective-permute-start(bf16[1024,1792]{1,0:T(8,128)(2,1)} %bitcast.23), channel_id=1, source_target_pairs={{0,16},{16,0},{32,48},{48,32},{64,80},{80,64},{96,112},{112,96},{1... | collective-permute-start | bytes 11010056 | tf_op jit(solution)/shard_map/ppermute | solution.py:85
  225.7 6.4 %copy-start.8 = (bf16[1792,1024]{1,0:T(8,128)(2,1)S(1)}, bf16[1792,1024]{1,0:T(8,128)(2,1)}, u32[]{:S(2)}) copy-start(bf16[1792,1024]{1,0:T(8,128)(2,1)} %param.13) | copy-start | bytes 11010052
  (1 other events, 1.8 us)
Sparse Core Ops, SparseCore 0:
  9.5 54.0 all-gather.1
  242.8 84.8 reduce-scatter.1
where the time goes:
time: 337 us; the launch traced here: 336 us
  waiting for transfers between devices  174 us (52%)
  blocking collectives  37.1 us (11%)
  matrix products  36.1 us (11%)
  local copies, waits for them, and re-layouts  31.7 us (9%)
  other arithmetic  23.2 us (7%)
  starting transfers between devices  20.6 us (6%)
  between operations  13.7 us (4%)
    ppermute x6, waiting for transfers between devices, row_reduce_scatter(): lax.ppermute(acc.astype(jnp.bfloat16), 'row', row_perm(n_row, direction))  54.7 us
    reduce_scatter x1, waiting for transfers between devices, on_device(): lax.psum_scatter(terms[:, :split], 'col', scatter_dimension=0, tiled=True)  47.7 us
    all_to_all x1, blocking collectives, on_device(): right = lax.all_to_all(right, 'col', 0, 0, tiled=False)  37.1 us
    all_gather x1, waiting for transfers between devices, on_device(): gathered = lax.all_gather(tokens, 'col', axis=0, tiled=True)  34.3 us
    ppermute x6, waiting for transfers between devices, row_all_gather(): held = lax.ppermute(held, 'row', row_perm(n_row, direction))  21.1 us
    dot_general x1, matrix products, row_reduce_scatter(): jnp.dot(keep, weights, preferred_element_type=jnp.float32)  14.5 us
    unnamed x20, local copies, waits for them, and re-layouts  13.9 us
    dot_general x1, matrix products, row_reduce_scatter(): jnp.dot(send, weights, preferred_element_type=jnp.float32)  13.4 us
  transfers between devices with their start and end apart: 16, of which 13 were waited for; matrix products, arithmetic and copies ran while one was open for 11% of the time, Pallas kernels for 0%

commit v1 on v0

--- a/solution.py
+++ b/solution.py
@@ -189,7 +189,8 @@
     )
     both_weights = jnp.concatenate([gate_pruned, up_pruned], axis=1)
     rows = tokens.shape[0] // CHUNKS
-    gathered = lax.all_gather(tokens, "col", axis=0, tiled=True)
+    copies = jnp.concatenate([tokens] * lax.axis_size("col"), axis=0)
+    gathered = lax.all_to_all(copies, "col", 0, 0, tiled=True)
     gathered = gathered.reshape(n_col, CHUNKS, rows, gathered.shape[1])
     outs = []
     previous = None

time: 337 us -> 365 us (1.083)
  local copies, waits for them, and re-layouts: 31.7 us -> 40.6 us
  starting transfers between devices: 20.6 us -> 28.7 us
  blocking collectives: 37.1 us -> 43 us
  waiting for transfers between devices: 174 us -> 179 us
    all_to_all x0 -> x1, waiting for transfers between devices: none -> 40 us  [on_device(): gathered = lax.all_to_all(copies, 'col', 0, 0, tiled=True)]
    all_gather x1 -> x0, waiting for transfers between devices: 34.3 us -> none  [on_device(): gathered = lax.all_gather(tokens, 'col', axis=0, tiled=True)]
    unnamed x20 -> x39, local copies, waits for them, and re-layouts: 13.9 us -> 22.8 us
    all_to_all x0 -> x1, starting transfers between devices: none -> 8.04 us  [on_device(): gathered = lax.all_to_all(copies, 'col', 0, 0, tiled=True)]
    all_to_all x1, blocking collectives: 37.1 us -> 43 us  [on_device(): right = lax.all_to_all(right, 'col', 0, 0, tiled=False)]
  transfers between devices with their start and end apart: 16 -> 16, of which waited for: 13 -> 13; matrix products, arithmetic and copies ran while one was open for 11% -> 10% of each run, Pallas kernels for 0% -> 0%
where the time goes in v1:
time: 365 us
  waiting for transfers between devices  179 us (49%)
  blocking collectives  43 us (12%)
  local copies, waits for them, and re-layouts  40.6 us (11%)
  matrix products  36.1 us (10%)
  starting transfers between devices  28.7 us (8%)
  other arithmetic  23.1 us (6%)
  between operations  13.8 us (4%)
    ppermute x6, waiting for transfers between devices, row_reduce_scatter(): lax.ppermute(acc.astype(jnp.bfloat16), 'row', row_perm(n_row, direction))  54.9 us
    reduce_scatter x1, waiting for transfers between devices, on_device(): lax.psum_scatter(terms[:, :split], 'col', scatter_dimension=0, tiled=True)  47.7 us
    all_to_all x1, blocking collectives, on_device(): right = lax.all_to_all(right, 'col', 0, 0, tiled=False)  43 us
    all_to_all x1, waiting for transfers between devices, on_device(): gathered = lax.all_to_all(copies, 'col', 0, 0, tiled=True)  40 us
    unnamed x39, local copies, waits for them, and re-layouts  22.8 us
    ppermute x6, waiting for transfers between devices, row_all_gather(): held = lax.ppermute(held, 'row', row_perm(n_row, direction))  21.2 us
    dot_general x1, matrix products, row_reduce_scatter(): jnp.dot(keep, weights, preferred_element_type=jnp.float32)  14.5 us
    dot_general x1, matrix products, row_reduce_scatter(): jnp.dot(send, weights, preferred_element_type=jnp.float32)  13.4 us
  transfers between devices with their start and end apart: 16, of which 13 were waited for; matrix products, arithmetic and copies ran while one was open for 10% of the time, Pallas kernels for 0%

profile of v1, /device:TPU:0, one launch (start us, length us, event | category | flops | bytes accessed | tf_op | source)
XLA Modules:
  0.0 364.5 jit_solution(1174572440824380409)
XLA Ops:
  15.6 8.0 %all-to-all-start = ((bf16[16,128,1024]{2,1,0:T(8,128)(2,1)}), bf16[16,128,1024]{2,1,0:T(8,128)(2,1)}, u32[]{:S(2)}, u32[]{:S(2)}) async-start(bf16[16,128,1024]{2,1,0:T(8,128)(2,1)} %bitcast.81), calls=%async_computation | async-start | bytes 8388608 | tf_op jit(solution)/shard_map/all_to_all | solution.py:193
  23.7 6.0 %copy.14 = bf16[1024,1792]{0,1:T(8,128)(2,1)} copy(bf16[1024,1792]{1,0:T(8,128)(2,1)} %param.12) | data formatting | bytes 7340032 | tf_op args[2]
  29.7 6.0 %copy.13 = bf16[1024,1792]{0,1:T(8,128)(2,1)} copy(bf16[1024,1792]{1,0:T(8,128)(2,1)} %param.11) | data formatting | bytes 7340032 | tf_op args[1]
  37.1 5.0 %bitcast_select_fusion.1 = bf16[1024,1792]{0,1:T(8,128)(2,1)} fusion(bf16[1024,1792]{0,1:T(8,128)(2,1)} %copy.14, pred[224,8,8,128]{3,2,1,0:T(8,128)(4,1)S(1)} %bitcast.79), kind=kLoop, calls=%fused_computation.5 | loop fusion | flops 1835008 | bytes 9175040 | tf_op jit(solution)/shard_map/jit(_where)/select_n | solution.py:25
  45.5 40.0 %all-to-all-done = bf16[16,128,1024]{2,1,0:T(8,128)(2,1)} async-done(((bf16[16,128,1024]{2,1,0:T(8,128)(2,1)}), bf16[16,128,1024]{2,1,0:T(8,128)(2,1)}, u32[]{:S(2)}, u32[]{:S(2)}) %all-to-all-start) | async-done | bytes 4194336 | tf_op jit(solution)/shard_map/all_to_all | solution.py:193
  85.5 13.4 %convolution_convert_fusion = bf16[1024,3584]{1,0:T(8,128)(2,1)} fusion(bf16[1024,1792]{0,1:T(8,128)(2,1)} %bitcast_select_fusion.1, bf16[1024,1792]{0,1:T(8,128)(2,1)} %bitcast_select_fusion.2, bf16[2,1024,1024]{2,1,0:T(8,128)(2,1)} %bitcast.1, s32[]{:T(128)S(6)} %select_n.138), kind=kOutput, calls=%fused_computation.1 | convolution fusion | flops 7534542848 | bytes 16777220 | tf_op jit(solution)/shard_map/dot_general | solution.py:44
  98.9 12.0 %collective-permute-done = bf16[1024,3584]{1,0:T(8,128)(2,1)} collective-permute-done((bf16[1024,3584]{1,0:T(8,128)(2,1)}, bf16[1024,3584]{1,0:T(8,128)(2,1)}, u32[]{:S(2)}, u32[]{:S(2)}) %collective-permute-start) | collective-permute-done | bytes 7340064 | tf_op jit(solution)/shard_map/ppermute | solution.py:46
  110.9 14.5 %add_convert_fusion = bf16[1024,3584]{1,0:T(8,128)(2,1)} fusion(bf16[1024,3584]{1,0:T(8,128)(2,1)} %collective-permute-done, bf16[1024,1792]{0,1:T(8,128)(2,1)} %bitcast_select_fusion.1, bf16[1024,1792]{0,1:T(8,128)(2,1)} %bitcast_select_fusion.2, bf16[2,1024,1024]{2,1,0:T(8,128)(2,1)} %bitcast.1, s32[]{:T(128)S(6)} %select_n.135), kind=kOutput, calls=%fused_computation | convolution fusion | flops 7549222912 | bytes 24117252 | tf_op jit(solution)/shard_map/dot_general | solution.py:47
  125.4 5.4 %fusion.22 = (bf16[4,256,1792]{2,1,0:T(8,128)(2,1)S(1)}, bf16[4,256,1792]{2,1,0:T(8,128)(2,1)}) fusion(bf16[4,256,3584]{2,1,0:T(8,128)(2,1)} %bitcast.77), kind=kLoop, calls=%fused_computation.75 | loop fusion | bytes 14680064 | tf_op jit(solution)/shard_map/slice | solution.py:55
  138.2 18.2 %collective-permute-done.1 = bf16[256,1792]{1,0:T(8,128)(2,1)S(1)} collective-permute-done((bf16[256,1792]{1,0:T(8,128)(2,1)S(1)}, bf16[256,1792]{1,0:T(8,128)(2,1)S(1)}, u32[]{:S(2)}, u32[]{:S(2)}) %collective-permute-start.1) | collective-permute-done | bytes 917536 | tf_op jit(solution)/shard_map/ppermute | solution.py:59
  164.2 16.5 %collective-permute-done.2 = bf16[256,1792]{1,0:T(8,128)(2,1)S(1)} collective-permute-done((bf16[256,1792]{1,0:T(8,128)(2,1)S(1)}, bf16[256,1792]{1,0:T(8,128)(2,1)S(1)}, u32[]{:S(2)}, u32[]{:S(2)}) %collective-permute-start.2) | collective-permute-done | bytes 917536 | tf_op jit(solution)/shard_map/ppermute | solution.py:59
  186.1 3.7 %collective-permute-start.6 = (bf16[256,1792]{1,0:T(8,128)(2,1)}, bf16[256,1792]{1,0:T(8,128)(2,1)S(1)}, u32[]{:S(2)}, u32[]{:S(2)}) collective-permute-start(bf16[256,1792]{1,0:T(8,128)(2,1)} %fusion.6), channel_id=1, source_target_pairs={{0,96},{16,112},{32,0},{48,16},{64,32},{80,48},{96,64},{112,80},{1... | collective-permute-start | bytes 2752520 | tf_op jit(solution)/shard_map/ppermute | solution.py:59
  189.8 14.3 %collective-permute-done.3 = bf16[256,1792]{1,0:T(8,128)(2,1)S(1)} collective-permute-done((bf16[256,1792]{1,0:T(8,128)(2,1)S(1)}, bf16[256,1792]{1,0:T(8,128)(2,1)S(1)}, u32[]{:S(2)}, u32[]{:S(2)}) %collective-permute-start.3) | collective-permute-done | bytes 917536 | tf_op jit(solution)/shard_map/ppermute | solution.py:59
  204.1 4.0 %collective-permute-done.6 = bf16[256,1792]{1,0:T(8,128)(2,1)S(1)} collective-permute-done((bf16[256,1792]{1,0:T(8,128)(2,1)}, bf16[256,1792]{1,0:T(8,128)(2,1)S(1)}, u32[]{:S(2)}, u32[]{:S(2)}) %collective-permute-start.6) | collective-permute-done | bytes 917536 | tf_op jit(solution)/shard_map/ppermute | solution.py:59
  210.5 3.7 %collective-permute-start.10 = (bf16[256,896]{1,0:T(8,128)(2,1)S(1)}, bf16[256,896]{1,0:T(8,128)(2,1)S(1)}, u32[]{:S(2)}, u32[]{:S(2)}) collective-permute-start(bf16[256,896]{1,0:T(8,128)(2,1)S(1)} %get-tuple-element.10), channel_id=1, source_target_pairs={{0,96},{16,112},{32,0},{48,16},{64,32},{80,48},{96,64},{112,80},{1... | collective-permute-start | bytes 1376264 | tf_op jit(solution)/shard_map/ppermute | solution.py:78
  214.6 7.6 %collective-permute-done.7 = bf16[256,896]{1,0:T(8,128)(2,1)S(1)} collective-permute-done((bf16[256,896]{1,0:T(8,128)(2,1)S(1)}, bf16[256,896]{1,0:T(8,128)(2,1)S(1)}, u32[]{:S(2)}, u32[]{:S(2)}) %collective-permute-start.7) | collective-permute-done | bytes 458784 | tf_op jit(solution)/shard_map/ppermute | solution.py:78
  222.2 3.2 collective-permute-start.11
  225.5 7.3 %collective-permute-done.8 = bf16[256,896]{1,0:T(8,128)(2,1)S(1)} collective-permute-done((bf16[256,896]{1,0:T(8,128)(2,1)S(1)}, bf16[256,896]{1,0:T(8,128)(2,1)S(1)}, u32[]{:S(2)}, u32[]{:S(2)}) %collective-permute-start.8) | collective-permute-done | bytes 458784 | tf_op jit(solution)/shard_map/ppermute | solution.py:78
  232.8 3.2 collective-permute-start.12
  236.2 6.3 %collective-permute-done.9 = bf16[256,896]{1,0:T(8,128)(2,1)S(1)} collective-permute-done((bf16[256,896]{1,0:T(8,128)(2,1)S(1)}, bf16[256,896]{1,0:T(8,128)(2,1)S(1)}, u32[]{:S(2)}, u32[]{:S(2)}) %collective-permute-start.9) | collective-permute-done | bytes 458784 | tf_op jit(solution)/shard_map/ppermute | solution.py:78
  248.1 3.4 collective-permute-done.13
  254.5 8.2 %convolution_convert_fusion.2 = bf16[2048,1024]{1,0:T(8,128)(2,1)S(1)} fusion(bf16[2048,1792]{1,0:T(8,128)(2,1)S(1)} %bitcast.78, bf16[1792,1024]{1,0:T(8,128)(2,1)S(1)} %copy-done.10, pred[224,8,8,128]{3,2,1,0:T(8,128)(4,1)S(1)} %bitcast.82), kind=kOutput, calls=%fused_computation.7 | convolution fusion | flops 7520124928 | bytes 17039360 | tf_op jit(solution)/shard_map/dot_general | solution.py:202
  265.1 43.0 %all_to_all.14 = bf16[16,128,512]{2,1,0:T(8,128)(2,1)S(1)} all-to-all(bf16[16,128,512]{2,1,0:T(8,128)(2,1)} %bitcast.76), channel_id=1, replica_groups=mesh['row'=8,'col'=16] {'col'}, dimensions={0} | all-to-all | bytes 4194304 | tf_op jit(solution)/shard_map/all_to_all | solution.py:212
  308.4 47.7 %reduce-scatter.2.cloned.1.call-done = bf16[128,512]{1,0:T(8,128)(2,1)} async-done(((bf16[2048,512]{1,0:T(8,128)(2,1)}), bf16[128,512]{1,0:T(8,128)(2,1)}) %reduce-scatter.2.cloned.1.call-update) | async-done | bytes 131088 | tf_op jit(solution)/shard_map/reduce_scatter | solution.py:210
  (92 shorter events, 50.1 us)
Async XLA Ops:
  6.5 6.9 %copy-start = (bf16[128,1024]{1,0:T(8,128)(2,1)S(1)}, bf16[128,1024]{1,0:T(8,128)(2,1)}, u32[]{:S(2)}) copy-start(bf16[128,1024]{1,0:T(8,128)(2,1)} %param.10) | copy-start | bytes 786436
  15.6 69.9 %all-to-all-start = ((bf16[16,128,1024]{2,1,0:T(8,128)(2,1)}), bf16[16,128,1024]{2,1,0:T(8,128)(2,1)}, u32[]{:S(2)}, u32[]{:S(2)}) async-start(bf16[16,128,1024]{2,1,0:T(8,128)(2,1)} %bitcast.81), calls=%async_computation | async-start | bytes 8388608 | tf_op jit(solution)/shard_map/all_to_all | solution.py:193
  23.7 332.4 %reduce-scatter.2.cloned.1.call-start = ((), (), s32[]{:S(2)}) async-start(), calls=%async_computation.3 | async-start | bytes 2228224 | tf_op jit(solution)/shard_map/reduce_scatter | solution.py:210
  29.7 6.0 %copy-start.7 = (s32[14]{0:T(128)S(1)}, s32[14]{0:T(128)}, u32[]{:S(2)}) copy-start(s32[14]{0:T(128)} %param.17) | copy-start | bytes 172
  29.7 6.1 %copy-start.5 = (s32[14,48]{1,0:T(8,128)S(1)}, s32[14,48]{1,0:T(8,128)}, u32[]{:S(2)}) copy-start(s32[14,48]{1,0:T(8,128)} %param.16) | copy-start | bytes 8068
  29.7 6.1 %copy-start.6 = (s32[14,48]{1,0:T(8,128)S(1)}, s32[14,48]{1,0:T(8,128)}, u32[]{:S(2)}) copy-start(s32[14,48]{1,0:T(8,128)} %param.14) | copy-start | bytes 8068
  29.7 6.4 %copy-start.8 = (s32[14]{0:T(128)S(1)}, s32[14]{0:T(128)}, u32[]{:S(2)}) copy-start(s32[14]{0:T(128)} %param.15) | copy-start | bytes 172
  37.1 5.6 %copy-start.2 = (bf16[1024,1792]{0,1:T(8,128)(2,1)S(1)}, bf16[1024,1792]{0,1:T(8,128)(2,1)}, u32[]{:S(2)}) copy-start(bf16[1024,1792]{0,1:T(8,128)(2,1)} %copy.13) | copy-start | bytes 11010052
  98.9 12.0 %collective-permute-start = (bf16[1024,3584]{1,0:T(8,128)(2,1)}, bf16[1024,3584]{1,0:T(8,128)(2,1)}, u32[]{:S(2)}, u32[]{:S(2)}) collective-permute-start(bf16[1024,3584]{1,0:T(8,128)(2,1)} %convolution_convert_fusion), channel_id=1, source_target_pairs={{0,16},{16,0},{32,48},{48,32},{64,80},{80,64},{96,112},{112,96},{1... | collective-permute-start | bytes 22020104 | tf_op jit(solution)/shard_map/ppermute | solution.py:46
  132.7 23.7 %collective-permute-start.1 = (bf16[256,1792]{1,0:T(8,128)(2,1)S(1)}, bf16[256,1792]{1,0:T(8,128)(2,1)S(1)}, u32[]{:S(2)}, u32[]{:S(2)}) collective-permute-start(bf16[256,1792]{1,0:T(8,128)(2,1)S(1)} %dynamic-slice_bitcast_fusion.1), channel_id=1, source_target_pairs={{0,32},{16,48},{32,64},{48,80},{64,96},{80,112},{96,0},{112,16},{1... | collective-permute-start | bytes 2752520 | tf_op jit(solution)/shard_map/ppermute | solution.py:59
  136.6 22.3 %collective-permute-start.4 = (bf16[256,1792]{1,0:T(8,128)(2,1)}, bf16[256,1792]{1,0:T(8,128)(2,1)S(1)}, u32[]{:S(2)}, u32[]{:S(2)}) collective-permute-start(bf16[256,1792]{1,0:T(8,128)(2,1)} %dynamic-slice_bitcast_fusion), channel_id=1, source_target_pairs={{0,96},{16,112},{32,0},{48,16},{64,32},{80,48},{96,64},{112,80},{1... | collective-permute-start | bytes 2752520 | tf_op jit(solution)/shard_map/ppermute | solution.py:59
  157.8 22.9 %collective-permute-start.2 = (bf16[256,1792]{1,0:T(8,128)(2,1)S(1)}, bf16[256,1792]{1,0:T(8,128)(2,1)S(1)}, u32[]{:S(2)}, u32[]{:S(2)}) collective-permute-start(bf16[256,1792]{1,0:T(8,128)(2,1)S(1)} %fusion.9), channel_id=1, source_target_pairs={{0,32},{16,48},{32,64},{48,80},{64,96},{80,112},{96,0},{112,16},{1... | collective-permute-start | bytes 2752520 | tf_op jit(solution)/shard_map/ppermute | solution.py:59
  161.3 22.2 %collective-permute-start.5 = (bf16[256,1792]{1,0:T(8,128)(2,1)}, bf16[256,1792]{1,0:T(8,128)(2,1)}, u32[]{:S(2)}, u32[]{:S(2)}) collective-permute-start(bf16[256,1792]{1,0:T(8,128)(2,1)} %fusion.7), channel_id=1, source_target_pairs={{0,96},{16,112},{32,0},{48,16},{64,32},{80,48},{96,64},{112,80},{1... | collective-permute-start | bytes 2752520 | tf_op jit(solution)/shard_map/ppermute | solution.py:59
  182.1 22.0 %collective-permute-start.3 = (bf16[256,1792]{1,0:T(8,128)(2,1)S(1)}, bf16[256,1792]{1,0:T(8,128)(2,1)S(1)}, u32[]{:S(2)}, u32[]{:S(2)}) collective-permute-start(bf16[256,1792]{1,0:T(8,128)(2,1)S(1)} %fusion.8), channel_id=1, source_target_pairs={{0,32},{16,48},{32,64},{48,80},{64,96},{80,112},{96,0},{112,16},{1... | collective-permute-start | bytes 2752520 | tf_op jit(solution)/shard_map/ppermute | solution.py:59
  186.1 22.0 %collective-permute-start.6 = (bf16[256,1792]{1,0:T(8,128)(2,1)}, bf16[256,1792]{1,0:T(8,128)(2,1)S(1)}, u32[]{:S(2)}, u32[]{:S(2)}) collective-permute-start(bf16[256,1792]{1,0:T(8,128)(2,1)} %fusion.6), channel_id=1, source_target_pairs={{0,96},{16,112},{32,0},{48,16},{64,32},{80,48},{96,64},{112,80},{1... | collective-permute-start | bytes 2752520 | tf_op jit(solution)/shard_map/ppermute | solution.py:59
  210.4 11.7 %collective-permute-start.7 = (bf16[256,896]{1,0:T(8,128)(2,1)S(1)}, bf16[256,896]{1,0:T(8,128)(2,1)S(1)}, u32[]{:S(2)}, u32[]{:S(2)}) collective-permute-start(bf16[256,896]{1,0:T(8,128)(2,1)S(1)} %get-tuple-element.9), channel_id=1, source_target_pairs={{0,32},{16,48},{32,64},{48,80},{64,96},{80,112},{96,0},{112,16},{1... | collective-permute-start | bytes 1376264 | tf_op jit(solution)/shard_map/ppermute | solution.py:78
  210.5 11.7 %collective-permute-start.10 = (bf16[256,896]{1,0:T(8,128)(2,1)S(1)}, bf16[256,896]{1,0:T(8,128)(2,1)S(1)}, u32[]{:S(2)}, u32[]{:S(2)}) collective-permute-start(bf16[256,896]{1,0:T(8,128)(2,1)S(1)} %get-tuple-element.10), channel_id=1, source_target_pairs={{0,96},{16,112},{32,0},{48,16},{64,32},{80,48},{96,64},{112,80},{1... | collective-permute-start | bytes 1376264 | tf_op jit(solution)/shard_map/ppermute | solution.py:78
  222.2 10.7 %collective-permute-start.8 = (bf16[256,896]{1,0:T(8,128)(2,1)S(1)}, bf16[256,896]{1,0:T(8,128)(2,1)S(1)}, u32[]{:S(2)}, u32[]{:S(2)}) collective-permute-start(bf16[256,896]{1,0:T(8,128)(2,1)S(1)} %collective-permute-done.7), channel_id=1, source_target_pairs={{0,32},{16,48},{32,64},{48,80},{64,96},{80,112},{96,0},{112,16},{1... | collective-permute-start | bytes 1376264 | tf_op jit(solution)/shard_map/ppermute | solution.py:78
  222.2 10.7 %collective-permute-start.11 = (bf16[256,896]{1,0:T(8,128)(2,1)S(1)}, bf16[256,896]{1,0:T(8,128)(2,1)S(1)}, u32[]{:S(2)}, u32[]{:S(2)}) collective-permute-start(bf16[256,896]{1,0:T(8,128)(2,1)S(1)} %collective-permute-done.10), channel_id=1, source_target_pairs={{0,96},{16,112},{32,0},{48,16},{64,32},{80,48},{96,64},{112,80},{1... | collective-permute-start | bytes 1376264 | tf_op jit(solution)/shard_map/ppermute | solution.py:78
  232.8 9.7 %collective-permute-start.9 = (bf16[256,896]{1,0:T(8,128)(2,1)S(1)}, bf16[256,896]{1,0:T(8,128)(2,1)S(1)}, u32[]{:S(2)}, u32[]{:S(2)}) collective-permute-start(bf16[256,896]{1,0:T(8,128)(2,1)S(1)} %collective-permute-done.8), channel_id=1, source_target_pairs={{0,32},{16,48},{32,64},{48,80},{64,96},{80,112},{96,0},{112,16},{1... | collective-permute-start | bytes 1376264 | tf_op jit(solution)/shard_map/ppermute | solution.py:78
  232.8 9.7 %collective-permute-start.12 = (bf16[256,896]{1,0:T(8,128)(2,1)S(1)}, bf16[256,896]{1,0:T(8,128)(2,1)S(1)}, u32[]{:S(2)}, u32[]{:S(2)}) collective-permute-start(bf16[256,896]{1,0:T(8,128)(2,1)S(1)} %collective-permute-done.11), channel_id=1, source_target_pairs={{0,96},{16,112},{32,0},{48,16},{64,32},{80,48},{96,64},{112,80},{1... | collective-permute-start | bytes 1376264 | tf_op jit(solution)/shard_map/ppermute | solution.py:78
  242.7 2.1 copy-start.4
  244.7 6.8 %collective-permute-start.13 = (bf16[1024,1792]{1,0:T(8,128)(2,1)}, bf16[1024,1792]{1,0:T(8,128)(2,1)}, u32[]{:S(2)}, u32[]{:S(2)}) collective-permute-start(bf16[1024,1792]{1,0:T(8,128)(2,1)} %bitcast.24), channel_id=1, source_target_pairs={{0,16},{16,0},{32,48},{48,32},{64,80},{80,64},{96,112},{112,96},{1... | collective-permute-start | bytes 11010056 | tf_op jit(solution)/shard_map/ppermute | solution.py:85
  248.1 6.4 %copy-start.10 = (bf16[1792,1024]{1,0:T(8,128)(2,1)S(1)}, bf16[1792,1024]{1,0:T(8,128)(2,1)}, u32[]{:S(2)}) copy-start(bf16[1792,1024]{1,0:T(8,128)(2,1)} %param.13) | copy-start | bytes 11010052
  (3 other events, 5.9 us)
Sparse Core Ops, SparseCore 0:
  265.2 90.8 reduce-scatter.1
